TPU v7x, 128 devices: a whole 4x4x4 slice. The times are simulated.
128 devices in a mesh: pair: 2 (over x_hi), gx: 8 (over y, x_lo), gy: 8 (over z, core).
Axes of the slice: x: 4 (x_hi: 2, x_lo: 2; x = x_hi * 2 + x_lo), y: 4, z: 4, core: 2. Of those that a mesh axis runs over, the one named last changes fastest.
Arguments:
- sound_speed_sq: float32 [64, 64, 1024], P('gx', 'gy'), may hold values from 0.5 to 2
- wind_profile: float32 [3, 1024], replicated, may hold values from -0.6 to 0.6
- forward_field: bfloat16 [4, 4, 64, 64, 1024], P(None, None, 'gx', 'gy'), may hold values from -6 to 6
- adjoint_state: float32 [2, 4, 64, 64, 1024], P('pair', None, 'gx', 'gy'), may hold values from -0.3125 to 0.3125
- pair_counts: int32 [2], P('pair'), may hold values from 64 to 256, as said below
- source_cells: int32 [512, 3], P('pair'), may hold values from 0 to 1023, as said below
- receiver_cells: int32 [512, 3], P('pair'), may hold values from 0 to 1023, as said below
- residuals: float32 [512, 4], P('pair'), may hold values from -16 to 16
Outputs:
- kernels: float32 [4, 64, 64, 1024], P(None, 'gx', 'gy', 'pair')
- final_state: float32 [2, 4, 64, 64, 1024], P('pair', None, 'gx', 'gy')
Inputs may be any that keep to these rules, and one draw needn't show every extreme that they name: `pair_counts`: one group in every draw has exactly 256 live pairs. `source_cells`: columns are the cell along the first, second and third dimension, each within the grid. `receiver_cells`: columns are the cell along the first, second and third dimension, each within the grid; several pairs may share a cell.
All inputs are finite; a program needn't handle non-finite values.
Results may differ from a plain program's by a relative error of at most 0.00115.
Values may be sent and summed in bfloat16 or wider, within the bound.
A program may use at most 128 MiB of HBM per device.

v0:
```python
import jax
import jax.numpy as jnp
from jax import lax
from jax.sharding import PartitionSpec as P

step_length = 0.25


def extended(shard, sides, width):
    for axis, dim in sides:
        size, length = (lax.axis_size(axis), shard.shape[dim])
        up = [(i, (i + 1) % size) for i in range(size - 1)]
        down = [(j, i) for i, j in up]
        last = lax.slice_in_dim(shard, length - width, length, axis=dim)
        initial = lax.slice_in_dim(shard, 0, width, axis=dim)
        before = lax.ppermute(last, axis, up)
        after = lax.ppermute(initial, axis, down)
        shard = jnp.concatenate([before, shard, after], axis=dim)
    return shard


def central(padded):
    dims = padded.ndim
    east_diff = (padded[..., 2:, 1:-1, :] - padded[..., :-2, 1:-1, :]) * 0.5
    north_diff = (padded[..., 1:-1, 2:, :] - padded[..., 1:-1, :-2, :]) * 0.5
    center = padded[..., 1:-1, 1:-1, :]
    vertical = jnp.pad(center, [(0, 0)] * (dims - 1) + [(1, 1)])
    up_diff = (vertical[..., 2:] - vertical[..., :-2]) * 0.5
    return (east_diff, north_diff, up_diff, center)


def local_flat(cells, width_x, width_y, depth):
    local_x = cells[:, 0] - lax.axis_index("gx") * width_x
    local_y = cells[:, 1] - lax.axis_index("gy") * width_y
    inside = (local_x >= 0) & (local_x < width_x) & (local_y >= 0) & (local_y < width_y)
    flat = (
        jnp.clip(local_x, 0, width_x - 1) * width_y + jnp.clip(local_y, 0, width_y - 1)
    ) * depth + cells[:, 2]
    return (flat, inside.astype(jnp.float32))


def shards(
    sound_speed_sq,
    wind_profile,
    forward_field,
    adjoint_state,
    pair_counts,
    source_cells,
    receiver_cells,
    residuals,
):
    steps_total = forward_field.shape[0]
    width_x, width_y, depth = sound_speed_sq.shape
    slots = residuals.shape[0]
    east_wind = wind_profile[0]
    north_wind = wind_profile[1]
    vertical_wind = wind_profile[2]
    live = (jnp.arange(slots, dtype=jnp.int32) < pair_counts[0]).astype(jnp.float32)
    src_flat, src_inside = local_flat(source_cells, width_x, width_y, depth)
    rcv_flat, rcv_inside = local_flat(receiver_cells, width_x, width_y, depth)
    pressure_snaps = forward_field[:, 0].reshape(steps_total, -1)
    local_samples = (
        jnp.take(pressure_snaps, src_flat, axis=1).astype(jnp.float32) * src_inside[None, :]
    )
    samples = lax.psum(local_samples, ("gx", "gy"))
    state = adjoint_state[0]
    kernel_local = jnp.zeros((4, width_x, width_y, depth), jnp.float32)
    for step in range(steps_total):
        snap = steps_total - 1 - step
        amplitude = residuals[:, snap] * samples[snap] * live * rcv_inside
        injected = (
            jnp.zeros((width_x * width_y * depth,), jnp.float32)
            .at[rcv_flat]
            .add(amplitude)
            .reshape(width_x, width_y, depth)
        )
        padded = extended(state, (("gx", 1), ("gy", 2)), 1)
        east_diff, north_diff, up_diff, center = central(padded)
        pressure = center[0]
        velocity = center[1:]
        divergence = east_diff[1] + north_diff[2] + up_diff[3]
        p_new = (
            pressure
            + step_length
            * (
                sound_speed_sq * divergence
                + east_wind * east_diff[0]
                + north_wind * north_diff[0]
                + vertical_wind * up_diff[0]
            )
            + injected
        )
        p_padded = extended(p_new, (("gx", 0), ("gy", 1)), 1)
        p_east, p_north, p_up, unused_center = central(p_padded)
        gradient = jnp.stack([p_east, p_north, p_up])
        a_new = velocity + step_length * (
            gradient
            + east_wind * east_diff[1:]
            + north_wind * north_diff[1:]
            + vertical_wind * up_diff[1:]
        )
        forward_rim = extended(forward_field[snap], (("gx", 1), ("gy", 2)), 1).astype(jnp.float32)
        f_east, f_north, f_up, unused_forward = central(forward_rim)
        pieces = [p_new * (f_east[1] + f_north[2] + f_up[3])]
        for along in (f_east, f_north, f_up):
            pieces.append(
                p_new * along[0] + a_new[0] * along[1] + a_new[1] * along[2] + a_new[2] * along[3]
            )
        increment = jnp.stack(pieces)
        kernel_local = kernel_local + increment
        state = jnp.concatenate([p_new[None], a_new], axis=0)
    kernels = lax.psum_scatter(kernel_local, "pair", scatter_dimension=3, tiled=True)
    return (kernels, state[None])


def solution(mesh):
    in_specs = (
        P("gx", "gy", None),
        P(),
        P(None, None, "gx", "gy", None),
        P("pair", None, "gx", "gy", None),
        P("pair"),
        P("pair", None),
        P("pair", None),
        P("pair", None),
    )
    out_specs = (P(None, "gx", "gy", "pair"), P("pair", None, "gx", "gy", None))
    return jax.shard_map(shards, mesh=mesh, in_specs=in_specs, out_specs=out_specs, check_vma=False)
```

profile of v0, /device:TPU:1, one launch (start us, length us, event | category | flops | bytes accessed | tf_op | source)
XLA Modules:
  0.0 556.1 jit_solution(320897750737244086)
XLA Ops:
  7.2 1.8 slice_bitcast_fusion
  11.0 5.2 collective-permute-start.4
  17.0 3.7 collective-permute-start.1
  20.6 1.3 collective-permute-start
  23.9 1.9 slice.831
  26.9 13.0 %copy.11 = bf16[4,1,8,8,1024]{0,4,3,2,1:T(8,128)(2,1)} copy(bf16[4,1,8,8,1024]{4,3,2,1,0:T(8,128)(2,1)} %slice.831) | data formatting | bytes 1048576 | tf_op jit(solution)/shard_map/slice | solution.py:61
  40.0 8.7 %gather_fusion = bf16[256,4]{1,0:T(8,128)(2,1)S(1)} fusion(bf16[4,65536]{0,1:T(8,128)(2,1)} %bitcast.532, s32[1024]{0:T(1024)S(1)} %pad_clamp_fusion), kind=kCustom, calls=%fused_computation | custom fusion | bytes 5120 | tf_op jit(solution)/shard_map/jit(_take)/gather | solution.py:63
  48.8 278.8 %psum.7 = f32[4,256]{0,1:T(8,128)S(1)} all-reduce(f32[4,256]{0,1:T(8,128)S(1)} %multiply_bitcast_fusion), channel_id=1, replica_groups=mesh['pair'=2,'gx'=8,'gy'=8] {'gx','gy'}, use_global_device_ids=true, to_apply=%region_0.1 | all-reduce | flops 1024 | bytes 8192 | tf_op jit(solution)/shard_map/psum | solution.py:65
  332.6 2.2 scatter_custom_fusion
  335.5 2.2 scatter_custom_fusion.1
  338.5 2.2 scatter_custom_fusion.2
  341.4 2.8 scatter_custom_fusion.3
  345.2 1.3 collective-permute-start.16
  349.0 4.0 collective-permute-start.28
  355.5 4.0 collective-permute-start.40
  359.5 9.9 %collective-permute-start.7 = (bf16[4,10,1,1024]{3,2,1,0:T(2,128)(2,1)S(1)}, bf16[4,10,1,1024]{3,2,1,0:T(2,128)(2,1)S(1)}, u32[]{:S(2)}, u32[]{:S(2)}) collective-permute-start(bf16[4,10,1,1024]{3,2,1,0:T(2,128)(2,1)S(1)} %get-tuple-element.75), channel_id=1, source_target_pairs={{1,0},{2,1},{3,2},{4,3},{5,4},{6,5},{7,6},{9,8},{10,9},{11,10},{12... | collective-permute-start | bytes 245768 | tf_op jit(solution)/shard_map/ppermute | solution.py:17
  369.6 1.9 collective-permute-start.6
  371.5 2.4 collective-permute-start.19
  374.2 3.2 collective-permute-start.18
  377.3 1.9 collective-permute-start.31
  380.5 3.6 collective-permute-start.3
  384.1 2.1 collective-permute-start.2
  386.2 1.6 maximum_convert_fusion
  389.1 3.8 collective-permute-start.30
  392.9 1.9 collective-permute-start.43
  394.8 1.9 fusion.39
  397.1 2.5 collective-permute-start.9
  400.9 1.5 maximum_convert_fusion.1
  402.5 1.8 collective-permute-done.8
  404.4 5.1 collective-permute-start.11
  409.4 1.9 collective-permute-start.10
  412.0 2.8 collective-permute-done.10
  415.5 2.5 collective-permute-start.13
  420.0 2.7 collective-permute-start.42
  423.9 3.3 collective-permute-start.15
  427.3 1.9 collective-permute-start.14
  429.9 4.0 collective-permute-done.14
  435.4 2.5 collective-permute-start.21
  439.9 2.7 collective-permute-done.20
  442.6 3.2 collective-permute-start.23
  445.8 1.9 collective-permute-start.22
  448.5 2.7 collective-permute-done.22
  451.9 2.5 collective-permute-start.25
  456.3 3.8 collective-permute-done.24
  460.3 3.3 collective-permute-start.27
  463.7 2.1 collective-permute-start.26
  467.1 3.2 collective-permute-done.26
  471.8 2.6 collective-permute-start.33
  476.0 3.0 collective-permute-done.32
  479.1 3.2 collective-permute-start.35
  482.3 1.9 collective-permute-start.34
  484.4 3.2 collective-permute-done.34
  488.3 2.5 collective-permute-start.37
  492.8 3.8 collective-permute-done.36
  496.8 4.3 collective-permute-start.39
  501.1 1.9 collective-permute-start.38
  503.3 4.4 collective-permute-done.38
  509.2 2.2 collective-permute-start.45
  513.1 3.0 collective-permute-done.44
  516.1 3.2 collective-permute-start.47
  519.3 1.9 collective-permute-start.46
  521.4 3.2 collective-permute-done.46
  525.8 1.5 fusion.41
  528.4 20.9 %reduce-scatter.2.cloned.1.call-done = f32[4,8,8,512]{3,2,1,0:T(8,128)} async-done(((f32[4,8,8,1024]{3,2,1,0:T(8,128)}), f32[4,8,8,512]{3,2,1,0:T(8,128)}) %reduce-scatter.2.cloned.1.call-update) | async-done | bytes 524304 | tf_op jit(solution)/shard_map/reduce_scatter | solution.py:112
  (138 shorter events, 48.2 us)
Async XLA Ops:
  7.2 9.1 %copy-start = (f32[1,4,8,8,1024]{4,3,2,1,0:T(8,128)S(1)}, f32[1,4,8,8,1024]{4,3,2,1,0:T(8,128)}, u32[]{:S(2)}) copy-start(f32[1,4,8,8,1024]{4,3,2,1,0:T(8,128)} %param.11) | copy-start | bytes 3145732
  7.2 18.6 %copy-start.6 = (f32[256,4]{0,1:T(4,128)S(1)}, f32[256,4]{0,1:T(4,128)}, u32[]{:S(2)}) copy-start(f32[256,4]{0,1:T(4,128)} %param.15) | copy-start | bytes 12292
  7.2 19.2 %copy-start.5 = (s32[256,3]{0,1:T(4,128)S(1)}, s32[256,3]{0,1:T(4,128)}, u32[]{:S(2)}) copy-start(s32[256,3]{0,1:T(4,128)} %param.14) | copy-start | bytes 9220
  7.2 19.7 %copy-start.7 = (s32[256,3]{0,1:T(4,128)S(1)}, s32[256,3]{0,1:T(4,128)}, u32[]{:S(2)}) copy-start(s32[256,3]{0,1:T(4,128)} %param.13) | copy-start | bytes 9220
  7.2 542.1 %reduce-scatter.2.cloned.1.call-start = ((), (), s32[]{:S(2)}) async-start(), calls=%async_computation.1 | async-start | bytes 1572864 | tf_op jit(solution)/shard_map/reduce_scatter | solution.py:112
  9.7 335.5 %collective-permute-start.5 = (bf16[4,1,8,1024]{3,2,1,0:T(8,128)(2,1)}, bf16[4,1,8,1024]{3,2,1,0:T(8,128)(2,1)}, u32[]{:S(2)}, u32[]{:S(2)}) collective-permute-start(bf16[4,1,8,1024]{3,2,1,0:T(8,128)(2,1)} %get-tuple-element.83), channel_id=1, source_target_pairs={{8,0},{16,8},{24,16},{32,24},{40,32},{48,40},{56,48},{9,1},{17,9},... | collective-permute-start | bytes 196616 | tf_op jit(solution)/shard_map/ppermute | solution.py:17
  11.0 335.5 %collective-permute-start.4 = (bf16[4,1,8,1024]{3,2,1,0:T(8,128)(2,1)}, bf16[4,1,8,1024]{3,2,1,0:T(8,128)(2,1)}, u32[]{:S(2)}, u32[]{:S(2)}) collective-permute-start(bf16[4,1,8,1024]{3,2,1,0:T(8,128)(2,1)} %get-tuple-element.82), channel_id=1, source_target_pairs={{0,8},{8,16},{16,24},{24,32},{32,40},{40,48},{48,56},{1,9},{9,17},... | collective-permute-start | bytes 196616 | tf_op jit(solution)/shard_map/ppermute | solution.py:16
  17.0 357.2 %collective-permute-start.1 = (f32[4,1,8,1024]{3,2,1,0:T(8,128)}, f32[4,1,8,1024]{3,2,1,0:T(8,128)S(1)}, u32[]{:S(2)}, u32[]{:S(2)}) collective-permute-start(f32[4,1,8,1024]{3,2,1,0:T(8,128)} %get-tuple-element.66), channel_id=1, source_target_pairs={{0,8},{8,16},{16,24},{24,32},{32,40},{40,48},{48,56},{1,9},{9,17},... | collective-permute-start | bytes 393224 | tf_op jit(solution)/shard_map/ppermute | solution.py:16
  20.6 356.7 %collective-permute-start = (f32[4,1,8,1024]{3,2,1,0:T(8,128)}, f32[4,1,8,1024]{3,2,1,0:T(8,128)}, u32[]{:S(2)}, u32[]{:S(2)}) collective-permute-start(f32[4,1,8,1024]{3,2,1,0:T(8,128)} %get-tuple-element.67), channel_id=1, source_target_pairs={{8,0},{16,8},{24,16},{32,24},{40,32},{48,40},{56,48},{9,1},{17,9},... | collective-permute-start | bytes 393224 | tf_op jit(solution)/shard_map/ppermute | solution.py:17
  22.6 326.4 %collective-permute-start.17 = (bf16[4,1,8,1024]{3,2,1,0:T(8,128)(2,1)}, bf16[4,1,8,1024]{3,2,1,0:T(8,128)(2,1)}, u32[]{:S(2)}, u32[]{:S(2)}) collective-permute-start(bf16[4,1,8,1024]{3,2,1,0:T(8,128)(2,1)} %get-tuple-element.81), channel_id=1, source_target_pairs={{8,0},{16,8},{24,16},{32,24},{40,32},{48,40},{56,48},{9,1},{17,9},... | collective-permute-start | bytes 196616 | tf_op jit(solution)/shard_map/ppermute | solution.py:17
  345.2 7.8 %collective-permute-start.16 = (bf16[4,1,8,1024]{3,2,1,0:T(8,128)(2,1)}, bf16[4,1,8,1024]{3,2,1,0:T(8,128)(2,1)S(1)}, u32[]{:S(2)}, u32[]{:S(2)}) collective-permute-start(bf16[4,1,8,1024]{3,2,1,0:T(8,128)(2,1)} %get-tuple-element.80), channel_id=1, source_target_pairs={{0,8},{8,16},{16,24},{24,32},{32,40},{40,48},{48,56},{1,9},{9,17},... | collective-permute-start | bytes 196616 | tf_op jit(solution)/shard_map/ppermute | solution.py:16
  346.5 8.9 %collective-permute-start.29 = (bf16[4,1,8,1024]{3,2,1,0:T(8,128)(2,1)}, bf16[4,1,8,1024]{3,2,1,0:T(8,128)(2,1)S(1)}, u32[]{:S(2)}, u32[]{:S(2)}) collective-permute-start(bf16[4,1,8,1024]{3,2,1,0:T(8,128)(2,1)} %get-tuple-element.79), channel_id=1, source_target_pairs={{8,0},{16,8},{24,16},{32,24},{40,32},{48,40},{56,48},{9,1},{17,9},... | collective-permute-start | bytes 196616 | tf_op jit(solution)/shard_map/ppermute | solution.py:17
  349.0 10.5 %collective-permute-start.28 = (bf16[4,1,8,1024]{3,2,1,0:T(8,128)(2,1)}, bf16[4,1,8,1024]{3,2,1,0:T(8,128)(2,1)S(1)}, u32[]{:S(2)}, u32[]{:S(2)}) collective-permute-start(bf16[4,1,8,1024]{3,2,1,0:T(8,128)(2,1)} %get-tuple-element.78), channel_id=1, source_target_pairs={{0,8},{8,16},{16,24},{24,32},{32,40},{40,48},{48,56},{1,9},{9,17},... | collective-permute-start | bytes 196616 | tf_op jit(solution)/shard_map/ppermute | solution.py:16
  353.0 16.6 %collective-permute-start.41 = (bf16[4,1,8,1024]{3,2,1,0:T(8,128)(2,1)}, bf16[4,1,8,1024]{3,2,1,0:T(8,128)(2,1)S(1)}, u32[]{:S(2)}, u32[]{:S(2)}) collective-permute-start(bf16[4,1,8,1024]{3,2,1,0:T(8,128)(2,1)} %get-tuple-element.77), channel_id=1, source_target_pairs={{8,0},{16,8},{24,16},{32,24},{40,32},{48,40},{56,48},{9,1},{17,9},... | collective-permute-start | bytes 196616 | tf_op jit(solution)/shard_map/ppermute | solution.py:17
  355.5 16.0 %collective-permute-start.40 = (bf16[4,1,8,1024]{3,2,1,0:T(8,128)(2,1)}, bf16[4,1,8,1024]{3,2,1,0:T(8,128)(2,1)S(1)}, u32[]{:S(2)}, u32[]{:S(2)}) collective-permute-start(bf16[4,1,8,1024]{3,2,1,0:T(8,128)(2,1)} %get-tuple-element.76), channel_id=1, source_target_pairs={{0,8},{8,16},{16,24},{24,32},{32,40},{40,48},{48,56},{1,9},{9,17},... | collective-permute-start | bytes 196616 | tf_op jit(solution)/shard_map/ppermute | solution.py:16
  359.5 21.0 %collective-permute-start.7 = (bf16[4,10,1,1024]{3,2,1,0:T(2,128)(2,1)S(1)}, bf16[4,10,1,1024]{3,2,1,0:T(2,128)(2,1)S(1)}, u32[]{:S(2)}, u32[]{:S(2)}) collective-permute-start(bf16[4,10,1,1024]{3,2,1,0:T(2,128)(2,1)S(1)} %get-tuple-element.75), channel_id=1, source_target_pairs={{1,0},{2,1},{3,2},{4,3},{5,4},{6,5},{7,6},{9,8},{10,9},{11,10},{12... | collective-permute-start | bytes 245768 | tf_op jit(solution)/shard_map/ppermute | solution.py:17
  369.6 14.5 %collective-permute-start.6 = (bf16[4,10,1,1024]{3,2,1,0:T(2,128)(2,1)S(1)}, bf16[4,10,1,1024]{3,2,1,0:T(2,128)(2,1)S(1)}, u32[]{:S(2)}, u32[]{:S(2)}) collective-permute-start(bf16[4,10,1,1024]{3,2,1,0:T(2,128)(2,1)S(1)} %get-tuple-element.74), channel_id=1, source_target_pairs={{0,1},{1,2},{2,3},{3,4},{4,5},{5,6},{6,7},{8,9},{9,10},{10,11},{11... | collective-permute-start | bytes 245768 | tf_op jit(solution)/shard_map/ppermute | solution.py:16
  371.5 25.6 %collective-permute-start.19 = (bf16[4,10,1,1024]{3,2,1,0:T(2,128)(2,1)S(1)}, bf16[4,10,1,1024]{3,2,1,0:T(2,128)(2,1)S(1)}, u32[]{:S(2)}, u32[]{:S(2)}) collective-permute-start(bf16[4,10,1,1024]{3,2,1,0:T(2,128)(2,1)S(1)} %get-tuple-element.73), channel_id=1, source_target_pairs={{1,0},{2,1},{3,2},{4,3},{5,4},{6,5},{7,6},{9,8},{10,9},{11,10},{12... | collective-permute-start | bytes 245768 | tf_op jit(solution)/shard_map/ppermute | solution.py:17
  374.2 25.5 %collective-permute-start.18 = (bf16[4,10,1,1024]{3,2,1,0:T(2,128)(2,1)S(1)}, bf16[4,10,1,1024]{3,2,1,0:T(2,128)(2,1)S(1)}, u32[]{:S(2)}, u32[]{:S(2)}) collective-permute-start(bf16[4,10,1,1024]{3,2,1,0:T(2,128)(2,1)S(1)} %get-tuple-element.72), channel_id=1, source_target_pairs={{0,1},{1,2},{2,3},{3,4},{4,5},{5,6},{6,7},{8,9},{9,10},{10,11},{11... | collective-permute-start | bytes 245768 | tf_op jit(solution)/shard_map/ppermute | solution.py:16
  377.3 50.0 %collective-permute-start.31 = (bf16[4,10,1,1024]{3,2,1,0:T(2,128)(2,1)S(1)}, bf16[4,10,1,1024]{3,2,1,0:T(2,128)(2,1)S(1)}, u32[]{:S(2)}, u32[]{:S(2)}) collective-permute-start(bf16[4,10,1,1024]{3,2,1,0:T(2,128)(2,1)S(1)} %get-tuple-element.71), channel_id=1, source_target_pairs={{1,0},{2,1},{3,2},{4,3},{5,4},{6,5},{7,6},{9,8},{10,9},{11,10},{12... | collective-permute-start | bytes 245768 | tf_op jit(solution)/shard_map/ppermute | solution.py:17
  380.5 8.6 %collective-permute-start.3 = (f32[4,10,1,1024]{3,2,1,0:T(1,128)S(1)}, f32[4,10,1,1024]{3,2,1,0:T(1,128)S(1)}, u32[]{:S(2)}, u32[]{:S(2)}) collective-permute-start(f32[4,10,1,1024]{3,2,1,0:T(1,128)S(1)} %get-tuple-element.47), channel_id=1, source_target_pairs={{0,1},{1,2},{2,3},{3,4},{4,5},{5,6},{6,7},{8,9},{9,10},{10,11},{11... | collective-permute-start | bytes 491528 | tf_op jit(solution)/shard_map/ppermute | solution.py:16
  384.1 8.7 %collective-permute-start.2 = (f32[4,10,1,1024]{3,2,1,0:T(1,128)S(1)}, f32[4,10,1,1024]{3,2,1,0:T(1,128)S(1)}, u32[]{:S(2)}, u32[]{:S(2)}) collective-permute-start(f32[4,10,1,1024]{3,2,1,0:T(1,128)S(1)} %get-tuple-element.46), channel_id=1, source_target_pairs={{1,0},{2,1},{3,2},{4,3},{5,4},{6,5},{7,6},{9,8},{10,9},{11,10},{12... | collective-permute-start | bytes 491528 | tf_op jit(solution)/shard_map/ppermute | solution.py:17
  389.0 7.7 %copy-start.1 = (f32[8,8,1024]{2,1,0:T(8,128)S(1)}, f32[8,8,1024]{2,1,0:T(8,128)}, u32[]{:S(2)}) copy-start(f32[8,8,1024]{2,1,0:T(8,128)} %param.8) | copy-start | bytes 786436
  389.0 7.7 %copy-start.4 = (f32[8,8,1024]{2,1,0:T(8,128)S(1)}, f32[8,8,1024]{2,1,0:T(8,128)}, u32[]{:S(2)}) copy-start(f32[8,8,1024]{2,1,0:T(8,128)} %reshape.127) | copy-start | bytes 786436
  389.1 40.2 %collective-permute-start.30 = (bf16[4,10,1,1024]{3,2,1,0:T(2,128)(2,1)S(1)}, bf16[4,10,1,1024]{3,2,1,0:T(2,128)(2,1)S(1)}, u32[]{:S(2)}, u32[]{:S(2)}) collective-permute-start(bf16[4,10,1,1024]{3,2,1,0:T(2,128)(2,1)S(1)} %get-tuple-element.70), channel_id=1, source_target_pairs={{0,1},{1,2},{2,3},{3,4},{4,5},{5,6},{6,7},{8,9},{9,10},{10,11},{11... | collective-permute-start | bytes 245768 | tf_op jit(solution)/shard_map/ppermute | solution.py:16
  392.9 54.9 %collective-permute-start.43 = (bf16[4,10,1,1024]{3,2,1,0:T(2,128)(2,1)S(1)}, bf16[4,10,1,1024]{3,2,1,0:T(2,128)(2,1)S(1)}, u32[]{:S(2)}, u32[]{:S(2)}) collective-permute-start(bf16[4,10,1,1024]{3,2,1,0:T(2,128)(2,1)S(1)} %get-tuple-element.69), channel_id=1, source_target_pairs={{1,0},{2,1},{3,2},{4,3},{5,4},{6,5},{7,6},{9,8},{10,9},{11,10},{12... | collective-permute-start | bytes 245768 | tf_op jit(solution)/shard_map/ppermute | solution.py:17
  397.1 5.4 collective-permute-start.9
  399.6 4.7 collective-permute-start.8
  404.4 7.6 %collective-permute-start.11 = (f32[10,1,1024]{2,1,0:T(1,128)S(1)}, f32[10,1,1024]{2,1,0:T(1,128)S(1)}, u32[]{:S(2)}, u32[]{:S(2)}) collective-permute-start(f32[10,1,1024]{2,1,0:T(1,128)S(1)} %get-tuple-element.99), channel_id=1, source_target_pairs={{0,1},{1,2},{2,3},{3,4},{4,5},{5,6},{6,7},{8,9},{9,10},{10,11},{11... | collective-permute-start | bytes 122888 | tf_op jit(solution)/shard_map/ppermute | solution.py:16
  409.4 5.3 collective-permute-start.10
  415.5 4.5 collective-permute-start.13
  418.0 5.7 %collective-permute-start.12 = (f32[4,1,8,1024]{3,2,1,0:T(8,128)S(1)}, f32[4,1,8,1024]{3,2,1,0:T(8,128)S(1)}, u32[]{:S(2)}, u32[]{:S(2)}) collective-permute-start(f32[4,1,8,1024]{3,2,1,0:T(8,128)S(1)} %get-tuple-element.62), channel_id=1, source_target_pairs={{8,0},{16,8},{24,16},{32,24},{40,32},{48,40},{56,48},{9,1},{17,9},... | collective-permute-start | bytes 393224 | tf_op jit(solution)/shard_map/ppermute | solution.py:17
  420.0 27.8 %collective-permute-start.42 = (bf16[4,10,1,1024]{3,2,1,0:T(2,128)(2,1)S(1)}, bf16[4,10,1,1024]{3,2,1,0:T(2,128)(2,1)S(1)}, u32[]{:S(2)}, u32[]{:S(2)}) collective-permute-start(bf16[4,10,1,1024]{3,2,1,0:T(2,128)(2,1)S(1)} %get-tuple-element.68), channel_id=1, source_target_pairs={{0,1},{1,2},{2,3},{3,4},{4,5},{5,6},{6,7},{8,9},{9,10},{10,11},{11... | collective-permute-start | bytes 245768 | tf_op jit(solution)/shard_map/ppermute | solution.py:16
  423.9 6.0 %collective-permute-start.15 = (f32[4,10,1,1024]{3,2,1,0:T(1,128)S(1)}, f32[4,10,1,1024]{3,2,1,0:T(1,128)S(1)}, u32[]{:S(2)}, u32[]{:S(2)}) collective-permute-start(f32[4,10,1,1024]{3,2,1,0:T(1,128)S(1)} %get-tuple-element.43), channel_id=1, source_target_pairs={{0,1},{1,2},{2,3},{3,4},{4,5},{5,6},{6,7},{8,9},{9,10},{10,11},{11... | collective-permute-start | bytes 491528 | tf_op jit(solution)/shard_map/ppermute | solution.py:16
  427.3 6.6 %collective-permute-start.14 = (f32[4,10,1,1024]{3,2,1,0:T(1,128)S(1)}, f32[4,10,1,1024]{3,2,1,0:T(1,128)S(1)}, u32[]{:S(2)}, u32[]{:S(2)}) collective-permute-start(f32[4,10,1,1024]{3,2,1,0:T(1,128)S(1)} %get-tuple-element.42), channel_id=1, source_target_pairs={{1,0},{2,1},{3,2},{4,3},{5,4},{6,5},{7,6},{9,8},{10,9},{11,10},{12... | collective-permute-start | bytes 491528 | tf_op jit(solution)/shard_map/ppermute | solution.py:17
  429.9 5.1 copy-start.3
  435.4 4.5 collective-permute-start.21
  437.9 4.7 collective-permute-start.20
  442.6 5.8 %collective-permute-start.23 = (f32[10,1,1024]{2,1,0:T(1,128)S(1)}, f32[10,1,1024]{2,1,0:T(1,128)S(1)}, u32[]{:S(2)}, u32[]{:S(2)}) collective-permute-start(f32[10,1,1024]{2,1,0:T(1,128)S(1)} %get-tuple-element.95), channel_id=1, source_target_pairs={{0,1},{1,2},{2,3},{3,4},{4,5},{5,6},{6,7},{8,9},{9,10},{10,11},{11... | collective-permute-start | bytes 122888 | tf_op jit(solution)/shard_map/ppermute | solution.py:16
  445.8 5.3 collective-permute-start.22
  451.9 4.5 collective-permute-start.25
  454.4 5.7 %collective-permute-start.24 = (f32[4,1,8,1024]{3,2,1,0:T(8,128)S(1)}, f32[4,1,8,1024]{3,2,1,0:T(8,128)S(1)}, u32[]{:S(2)}, u32[]{:S(2)}) collective-permute-start(f32[4,1,8,1024]{3,2,1,0:T(8,128)S(1)} %get-tuple-element.57), channel_id=1, source_target_pairs={{8,0},{16,8},{24,16},{32,24},{40,32},{48,40},{56,48},{9,1},{17,9},... | collective-permute-start | bytes 393224 | tf_op jit(solution)/shard_map/ppermute | solution.py:17
  460.3 6.7 %collective-permute-start.27 = (f32[4,10,1,1024]{3,2,1,0:T(1,128)S(1)}, f32[4,10,1,1024]{3,2,1,0:T(1,128)S(1)}, u32[]{:S(2)}, u32[]{:S(2)}) collective-permute-start(f32[4,10,1,1024]{3,2,1,0:T(1,128)S(1)} %get-tuple-element.39), channel_id=1, source_target_pairs={{0,1},{1,2},{2,3},{3,4},{4,5},{5,6},{6,7},{8,9},{9,10},{10,11},{11... | collective-permute-start | bytes 491528 | tf_op jit(solution)/shard_map/ppermute | solution.py:16
  463.7 6.6 %collective-permute-start.26 = (f32[4,10,1,1024]{3,2,1,0:T(1,128)S(1)}, f32[4,10,1,1024]{3,2,1,0:T(1,128)S(1)}, u32[]{:S(2)}, u32[]{:S(2)}) collective-permute-start(f32[4,10,1,1024]{3,2,1,0:T(1,128)S(1)} %get-tuple-element.38), channel_id=1, source_target_pairs={{1,0},{2,1},{3,2},{4,3},{5,4},{6,5},{7,6},{9,8},{10,9},{11,10},{12... | collective-permute-start | bytes 491528 | tf_op jit(solution)/shard_map/ppermute | solution.py:17
  467.0 4.4 copy-start.2
  471.8 4.2 collective-permute-start.33
  474.4 4.7 collective-permute-start.32
  479.1 5.3 collective-permute-start.35
  482.3 5.3 collective-permute-start.34
  488.3 4.5 collective-permute-start.37
  490.9 5.7 %collective-permute-start.36 = (f32[4,1,8,1024]{3,2,1,0:T(8,128)S(1)}, f32[4,1,8,1024]{3,2,1,0:T(8,128)S(1)}, u32[]{:S(2)}, u32[]{:S(2)}) collective-permute-start(f32[4,1,8,1024]{3,2,1,0:T(8,128)S(1)} %get-tuple-element.52), channel_id=1, source_target_pairs={{8,0},{16,8},{24,16},{32,24},{40,32},{48,40},{56,48},{9,1},{17,9},... | collective-permute-start | bytes 393224 | tf_op jit(solution)/shard_map/ppermute | solution.py:17
  496.8 6.6 %collective-permute-start.39 = (f32[4,10,1,1024]{3,2,1,0:T(1,128)S(1)}, f32[4,10,1,1024]{3,2,1,0:T(1,128)S(1)}, u32[]{:S(2)}, u32[]{:S(2)}) collective-permute-start(f32[4,10,1,1024]{3,2,1,0:T(1,128)S(1)} %get-tuple-element.35), channel_id=1, source_target_pairs={{0,1},{1,2},{2,3},{3,4},{4,5},{5,6},{6,7},{8,9},{9,10},{10,11},{11... | collective-permute-start | bytes 491528 | tf_op jit(solution)/shard_map/ppermute | solution.py:16
  501.1 6.6 %collective-permute-start.38 = (f32[4,10,1,1024]{3,2,1,0:T(1,128)S(1)}, f32[4,10,1,1024]{3,2,1,0:T(1,128)S(1)}, u32[]{:S(2)}, u32[]{:S(2)}) collective-permute-start(f32[4,10,1,1024]{3,2,1,0:T(1,128)S(1)} %get-tuple-element.34), channel_id=1, source_target_pairs={{1,0},{2,1},{3,2},{4,3},{5,4},{6,5},{7,6},{9,8},{10,9},{11,10},{12... | collective-permute-start | bytes 491528 | tf_op jit(solution)/shard_map/ppermute | solution.py:17
  509.2 3.9 collective-permute-start.45
  511.4 4.7 collective-permute-start.44
  516.1 5.3 collective-permute-start.47
  519.3 5.3 collective-permute-start.46
Sparse Core Ops, SparseCore 0:
  527.4 21.7 reduce-scatter.1
where the time goes:
time: 559 us; the launch traced here: 556 us
  blocking collectives  279 us (50%)
  starting transfers between devices  124 us (22%)
  waiting for transfers between devices  64.3 us (12%)
  other arithmetic  39.6 us (7%)
  local copies, waits for them, and re-layouts  33.9 us (6%)
  between operations  15.8 us (3%)
    psum x1, blocking collectives, shards(): samples = lax.psum(local_samples, ('gx', 'gy'))  279 us
    ppermute x24, starting transfers between devices, extended(): before = lax.ppermute(last, axis, up)  76.4 us
    ppermute x24, starting transfers between devices, extended(): after = lax.ppermute(initial, axis, down)  47.4 us
    ppermute x24, waiting for transfers between devices, extended(): after = lax.ppermute(initial, axis, down)  42.7 us
    reduce_scatter x1, waiting for transfers between devices, shards(): lax.psum_scatter(kernel_local, 'pair', scatter_dimension=3, tiled=True)  20.9 us
    slice x2, local copies, waits for them, and re-layouts, shards(): pressure_snaps = forward_field[:, 0].reshape(steps_total, -1)  14.9 us
  transfers between devices with their start and end apart: 49, of which 18 were waited for; matrix products, arithmetic and copies ran while one was open for 11% of the time, Pallas kernels for 0%

commit v1 on v0

--- a/solution.py
+++ b/solution.py
@@ -62,7 +62,7 @@
     local_samples = (
         jnp.take(pressure_snaps, src_flat, axis=1).astype(jnp.float32) * src_inside[None, :]
     )
-    samples = lax.psum(local_samples, ("gx", "gy"))
+    samples = lax.psum(lax.psum(local_samples, "gx"), "gy")
     state = adjoint_state[0]
     kernel_local = jnp.zeros((4, width_x, width_y, depth), jnp.float32)
     for step in range(steps_total):

time: 559 us -> 347 us (0.62)
  blocking collectives: 279 us -> 64.4 us
    psum x1 -> x2, blocking collectives: 279 us -> 64.4 us  [shards(): samples = lax.psum(lax.psum(local_samples, 'gx'), 'gy')]
    ppermute x24, starting transfers between devices: 76.4 us -> 82.8 us  [extended(): before = lax.ppermute(last, axis, up)]
  transfers between devices with their start and end apart: 49 -> 49, of which waited for: 18 -> 18; matrix products, arithmetic and copies ran while one was open for 11% -> 19% of each run, Pallas kernels for 0% -> 0%
where the time goes in v1:
time: 347 us; the launch traced here: 344 us
  starting transfers between devices  127 us (37%)
  blocking collectives  64.4 us (19%)
  waiting for transfers between devices  63 us (18%)
  other arithmetic  39.7 us (11%)
  local copies, waits for them, and re-layouts  34 us (10%)
  between operations  15.8 us (5%)
    ppermute x24, starting transfers between devices, extended(): before = lax.ppermute(last, axis, up)  82.8 us
    psum x2, blocking collectives, shards(): samples = lax.psum(lax.psum(local_samples, 'gx'), 'gy')  64.4 us
    ppermute x24, starting transfers between devices, extended(): after = lax.ppermute(initial, axis, down)  44 us
    ppermute x24, waiting for transfers between devices, extended(): after = lax.ppermute(initial, axis, down)  43.3 us
    reduce_scatter x1, waiting for transfers between devices, shards(): lax.psum_scatter(kernel_local, 'pair', scatter_dimension=3, tiled=True)  19 us
    slice x2, local copies, waits for them, and re-layouts, shards(): pressure_snaps = forward_field[:, 0].reshape(steps_total, -1)  15 us
    scatter-add x4, other arithmetic, shards(): injected = jnp.zeros((width_x * width_y * depth,), jnp.float32).at[rcv_fl...  9.35 us
    gather x1, local copies, waits for them, and re-layouts, shards(): jnp.take(pressure_snaps, src_flat, axis=1).astype(jnp.float32)  8.65 us
  transfers between devices with their start and end apart: 49, of which 18 were waited for; matrix products, arithmetic and copies ran while one was open for 19% of the time, Pallas kernels for 0%

profile of v1, /device:TPU:1, one launch (start us, length us, event | category | flops | bytes accessed | tf_op | source)
XLA Modules:
  0.0 343.7 jit_solution(17728707361067257529)
XLA Ops:
  7.2 1.8 slice_bitcast_fusion
  11.0 5.2 %collective-permute-start.4 = (bf16[4,1,8,1024]{3,2,1,0:T(8,128)(2,1)}, bf16[4,1,8,1024]{3,2,1,0:T(8,128)(2,1)}, u32[]{:S(2)}, u32[]{:S(2)}) collective-permute-start(bf16[4,1,8,1024]{3,2,1,0:T(8,128)(2,1)} %get-tuple-element.82), channel_id=1, source_target_pairs={{0,8},{8,16},{16,24},{24,32},{32,40},{40,48},{48,56},{1,9},{9,17},... | collective-permute-start | bytes 196616 | tf_op jit(solution)/shard_map/ppermute | solution.py:16
  17.0 3.6 %collective-permute-start.1 = (f32[4,1,8,1024]{3,2,1,0:T(8,128)}, f32[4,1,8,1024]{3,2,1,0:T(8,128)S(1)}, u32[]{:S(2)}, u32[]{:S(2)}) collective-permute-start(f32[4,1,8,1024]{3,2,1,0:T(8,128)} %get-tuple-element.66), channel_id=1, source_target_pairs={{0,8},{8,16},{16,24},{24,32},{32,40},{40,48},{48,56},{1,9},{9,17},... | collective-permute-start | bytes 393224 | tf_op jit(solution)/shard_map/ppermute | solution.py:16
  23.9 1.9 slice.831
  26.9 13.2 %copy.11 = bf16[4,1,8,8,1024]{0,4,3,2,1:T(8,128)(2,1)} copy(bf16[4,1,8,8,1024]{4,3,2,1,0:T(8,128)(2,1)} %slice.831) | data formatting | bytes 1048576 | tf_op jit(solution)/shard_map/slice | solution.py:61
  40.1 8.7 %gather_fusion = bf16[256,4]{1,0:T(8,128)(2,1)S(1)} fusion(bf16[4,65536]{0,1:T(8,128)(2,1)} %bitcast.532, s32[1024]{0:T(1024)S(1)} %pad_clamp_fusion), kind=kCustom, calls=%fused_computation | custom fusion | bytes 5120 | tf_op jit(solution)/shard_map/jit(_take)/gather | solution.py:63
  48.9 32.7 %psum.14 = f32[4,256]{0,1:T(8,128)S(1)} all-reduce(f32[4,256]{0,1:T(8,128)S(1)} %multiply_bitcast_fusion), channel_id=1, replica_groups=mesh['pair'=2,'gx'=8,'gy'=8] {'gx'}, use_global_device_ids=true, to_apply=%region_0.1 | all-reduce | flops 1024 | bytes 8192 | tf_op jit(solution)/shard_map/psum | solution.py:65
  81.6 31.7 %psum.15 = f32[4,256]{0,1:T(8,128)S(1)} all-reduce(f32[4,256]{0,1:T(8,128)S(1)} %psum.14), channel_id=1, replica_groups=mesh['pair'=2,'gx'=8,'gy'=8] {'gy'}, use_global_device_ids=true, to_apply=%region_1.2 | all-reduce | flops 1024 | bytes 8192 | tf_op jit(solution)/shard_map/psum | solution.py:65
  116.5 1.3 select_select_fusion
  118.4 2.2 scatter_custom_fusion
  121.4 2.2 scatter_custom_fusion.1
  124.3 2.2 scatter_custom_fusion.2
  127.3 2.8 scatter_custom_fusion.3
  134.9 4.0 %collective-permute-start.28 = (bf16[4,1,8,1024]{3,2,1,0:T(8,128)(2,1)}, bf16[4,1,8,1024]{3,2,1,0:T(8,128)(2,1)S(1)}, u32[]{:S(2)}, u32[]{:S(2)}) collective-permute-start(bf16[4,1,8,1024]{3,2,1,0:T(8,128)(2,1)} %get-tuple-element.78), channel_id=1, source_target_pairs={{0,8},{8,16},{16,24},{24,32},{32,40},{40,48},{48,56},{1,9},{9,17},... | collective-permute-start | bytes 196616 | tf_op jit(solution)/shard_map/ppermute | solution.py:16
  141.3 4.0 %collective-permute-start.40 = (bf16[4,1,8,1024]{3,2,1,0:T(8,128)(2,1)}, bf16[4,1,8,1024]{3,2,1,0:T(8,128)(2,1)S(1)}, u32[]{:S(2)}, u32[]{:S(2)}) collective-permute-start(bf16[4,1,8,1024]{3,2,1,0:T(8,128)(2,1)} %get-tuple-element.76), channel_id=1, source_target_pairs={{0,8},{8,16},{16,24},{24,32},{32,40},{40,48},{48,56},{1,9},{9,17},... | collective-permute-start | bytes 196616 | tf_op jit(solution)/shard_map/ppermute | solution.py:16
  145.3 6.5 %collective-permute-start.7 = (bf16[4,10,1,1024]{3,2,1,0:T(2,128)(2,1)S(1)}, bf16[4,10,1,1024]{3,2,1,0:T(2,128)(2,1)S(1)}, u32[]{:S(2)}, u32[]{:S(2)}) collective-permute-start(bf16[4,10,1,1024]{3,2,1,0:T(2,128)(2,1)S(1)} %get-tuple-element.75), channel_id=1, source_target_pairs={{1,0},{2,1},{3,2},{4,3},{5,4},{6,5},{7,6},{9,8},{10,9},{11,10},{12... | collective-permute-start | bytes 245768 | tf_op jit(solution)/shard_map/ppermute | solution.py:17
  152.1 1.9 collective-permute-start.6
  154.0 2.4 collective-permute-start.19
  156.7 3.2 collective-permute-start.18
  159.8 1.9 collective-permute-start.31
  163.0 3.6 %collective-permute-start.3 = (f32[4,10,1,1024]{3,2,1,0:T(1,128)S(1)}, f32[4,10,1,1024]{3,2,1,0:T(1,128)S(1)}, u32[]{:S(2)}, u32[]{:S(2)}) collective-permute-start(f32[4,10,1,1024]{3,2,1,0:T(1,128)S(1)} %get-tuple-element.47), channel_id=1, source_target_pairs={{0,1},{1,2},{2,3},{3,4},{4,5},{5,6},{6,7},{8,9},{9,10},{10,11},{11... | collective-permute-start | bytes 491528 | tf_op jit(solution)/shard_map/ppermute | solution.py:16
  166.6 2.1 collective-permute-start.2
  168.7 1.6 maximum_convert_fusion
  171.6 3.8 %collective-permute-start.30 = (bf16[4,10,1,1024]{3,2,1,0:T(2,128)(2,1)S(1)}, bf16[4,10,1,1024]{3,2,1,0:T(2,128)(2,1)S(1)}, u32[]{:S(2)}, u32[]{:S(2)}) collective-permute-start(bf16[4,10,1,1024]{3,2,1,0:T(2,128)(2,1)S(1)} %get-tuple-element.70), channel_id=1, source_target_pairs={{0,1},{1,2},{2,3},{3,4},{4,5},{5,6},{6,7},{8,9},{9,10},{10,11},{11... | collective-permute-start | bytes 245768 | tf_op jit(solution)/shard_map/ppermute | solution.py:16
  175.4 1.9 collective-permute-start.43
  177.3 1.9 fusion.39
  179.6 4.3 %collective-permute-start.9 = (f32[1,8,1024]{2,1,0:T(8,128)S(1)}, f32[1,8,1024]{2,1,0:T(8,128)S(1)}, u32[]{:S(2)}, u32[]{:S(2)}) collective-permute-start(f32[1,8,1024]{2,1,0:T(8,128)S(1)} %get-tuple-element.110), channel_id=1, source_target_pairs={{0,8},{8,16},{16,24},{24,32},{32,40},{40,48},{48,56},{1,9},{9,17},... | collective-permute-start | bytes 98312 | tf_op jit(solution)/shard_map/ppermute | solution.py:16
  185.2 1.5 maximum_convert_fusion.1
  186.7 1.8 collective-permute-done.8
  188.6 5.1 %collective-permute-start.11 = (f32[10,1,1024]{2,1,0:T(1,128)S(1)}, f32[10,1,1024]{2,1,0:T(1,128)S(1)}, u32[]{:S(2)}, u32[]{:S(2)}) collective-permute-start(f32[10,1,1024]{2,1,0:T(1,128)S(1)} %get-tuple-element.99), channel_id=1, source_target_pairs={{0,1},{1,2},{2,3},{3,4},{4,5},{5,6},{6,7},{8,9},{9,10},{10,11},{11... | collective-permute-start | bytes 122888 | tf_op jit(solution)/shard_map/ppermute | solution.py:16
  193.7 1.9 collective-permute-start.10
  196.3 2.8 collective-permute-done.10
  199.7 2.5 collective-permute-start.13
  204.2 2.7 collective-permute-start.42
  208.3 3.3 collective-permute-start.15
  211.6 1.9 collective-permute-start.14
  214.2 4.0 %collective-permute-done.14 = f32[4,10,1,1024]{3,2,1,0:T(1,128)S(1)} collective-permute-done((f32[4,10,1,1024]{3,2,1,0:T(1,128)S(1)}, f32[4,10,1,1024]{3,2,1,0:T(1,128)S(1)}, u32[]{:S(2)}, u32[]{:S(2)}) %collective-permute-start.14) | collective-permute-done | bytes 163872 | tf_op jit(solution)/shard_map/ppermute | solution.py:17
  219.6 3.6 %collective-permute-start.21 = (f32[1,8,1024]{2,1,0:T(8,128)S(1)}, f32[1,8,1024]{2,1,0:T(8,128)S(1)}, u32[]{:S(2)}, u32[]{:S(2)}) collective-permute-start(f32[1,8,1024]{2,1,0:T(8,128)S(1)} %get-tuple-element.107), channel_id=1, source_target_pairs={{0,8},{8,16},{16,24},{24,32},{32,40},{40,48},{48,56},{1,9},{9,17},... | collective-permute-start | bytes 98312 | tf_op jit(solution)/shard_map/ppermute | solution.py:16
  225.2 2.8 collective-permute-done.20
  228.0 3.1 collective-permute-start.23
  231.1 1.9 collective-permute-start.22
  233.8 2.7 collective-permute-done.22
  237.2 4.3 %collective-permute-start.25 = (f32[4,1,8,1024]{3,2,1,0:T(8,128)S(1)}, f32[4,1,8,1024]{3,2,1,0:T(8,128)S(1)}, u32[]{:S(2)}, u32[]{:S(2)}) collective-permute-start(f32[4,1,8,1024]{3,2,1,0:T(8,128)S(1)} %get-tuple-element.56), channel_id=1, source_target_pairs={{0,8},{8,16},{16,24},{24,32},{32,40},{40,48},{48,56},{1,9},{9,17},... | collective-permute-start | bytes 393224 | tf_op jit(solution)/shard_map/ppermute | solution.py:16
  243.4 4.3 %collective-permute-done.24 = f32[4,1,8,1024]{3,2,1,0:T(8,128)S(1)} collective-permute-done((f32[4,1,8,1024]{3,2,1,0:T(8,128)S(1)}, f32[4,1,8,1024]{3,2,1,0:T(8,128)S(1)}, u32[]{:S(2)}, u32[]{:S(2)}) %collective-permute-start.24) | collective-permute-done | bytes 131104 | tf_op jit(solution)/shard_map/ppermute | solution.py:17
  247.9 3.1 collective-permute-start.27
  251.0 2.1 collective-permute-start.26
  254.4 3.2 collective-permute-done.26
  259.1 3.9 %collective-permute-start.33 = (f32[1,8,1024]{2,1,0:T(8,128)S(1)}, f32[1,8,1024]{2,1,0:T(8,128)S(1)}, u32[]{:S(2)}, u32[]{:S(2)}) collective-permute-start(f32[1,8,1024]{2,1,0:T(8,128)S(1)} %get-tuple-element.104), channel_id=1, source_target_pairs={{0,8},{8,16},{16,24},{24,32},{32,40},{40,48},{48,56},{1,9},{9,17},... | collective-permute-start | bytes 98312 | tf_op jit(solution)/shard_map/ppermute | solution.py:16
  264.6 3.0 collective-permute-done.32
  267.7 3.2 collective-permute-start.35
  270.9 1.9 collective-permute-start.34
  273.0 3.2 collective-permute-done.34
  276.9 3.5 %collective-permute-start.37 = (f32[4,1,8,1024]{3,2,1,0:T(8,128)S(1)}, f32[4,1,8,1024]{3,2,1,0:T(8,128)S(1)}, u32[]{:S(2)}, u32[]{:S(2)}) collective-permute-start(f32[4,1,8,1024]{3,2,1,0:T(8,128)S(1)} %get-tuple-element.51), channel_id=1, source_target_pairs={{0,8},{8,16},{16,24},{24,32},{32,40},{40,48},{48,56},{1,9},{9,17},... | collective-permute-start | bytes 393224 | tf_op jit(solution)/shard_map/ppermute | solution.py:16
  282.4 3.8 %collective-permute-done.36 = f32[4,1,8,1024]{3,2,1,0:T(8,128)S(1)} collective-permute-done((f32[4,1,8,1024]{3,2,1,0:T(8,128)S(1)}, f32[4,1,8,1024]{3,2,1,0:T(8,128)S(1)}, u32[]{:S(2)}, u32[]{:S(2)}) %collective-permute-start.36) | collective-permute-done | bytes 131104 | tf_op jit(solution)/shard_map/ppermute | solution.py:17
  286.3 3.7 %collective-permute-start.39 = (f32[4,10,1,1024]{3,2,1,0:T(1,128)S(1)}, f32[4,10,1,1024]{3,2,1,0:T(1,128)S(1)}, u32[]{:S(2)}, u32[]{:S(2)}) collective-permute-start(f32[4,10,1,1024]{3,2,1,0:T(1,128)S(1)} %get-tuple-element.35), channel_id=1, source_target_pairs={{0,1},{1,2},{2,3},{3,4},{4,5},{5,6},{6,7},{8,9},{9,10},{10,11},{11... | collective-permute-start | bytes 491528 | tf_op jit(solution)/shard_map/ppermute | solution.py:16
  290.0 1.9 collective-permute-start.38
  292.3 4.4 %collective-permute-done.38 = f32[4,10,1,1024]{3,2,1,0:T(1,128)S(1)} collective-permute-done((f32[4,10,1,1024]{3,2,1,0:T(1,128)S(1)}, f32[4,10,1,1024]{3,2,1,0:T(1,128)S(1)}, u32[]{:S(2)}, u32[]{:S(2)}) %collective-permute-start.38) | collective-permute-done | bytes 163872 | tf_op jit(solution)/shard_map/ppermute | solution.py:17
  298.1 2.8 collective-permute-start.45
  302.6 3.0 collective-permute-done.44
  305.7 3.2 collective-permute-start.47
  308.8 1.9 collective-permute-start.46
  310.9 3.2 collective-permute-done.46
  315.4 1.5 fusion.41
  317.9 19.0 %reduce-scatter.2.cloned.1.call-done = f32[4,8,8,512]{3,2,1,0:T(8,128)} async-done(((f32[4,8,8,1024]{3,2,1,0:T(8,128)}), f32[4,8,8,512]{3,2,1,0:T(8,128)}) %reduce-scatter.2.cloned.1.call-update) | async-done | bytes 524304 | tf_op jit(solution)/shard_map/reduce_scatter | solution.py:112
  (139 shorter events, 49.6 us)
Async XLA Ops:
  7.2 9.1 %copy-start = (f32[1,4,8,8,1024]{4,3,2,1,0:T(8,128)S(1)}, f32[1,4,8,8,1024]{4,3,2,1,0:T(8,128)}, u32[]{:S(2)}) copy-start(f32[1,4,8,8,1024]{4,3,2,1,0:T(8,128)} %param.11) | copy-start | bytes 3145732
  7.2 18.6 %copy-start.6 = (f32[256,4]{0,1:T(4,128)S(1)}, f32[256,4]{0,1:T(4,128)}, u32[]{:S(2)}) copy-start(f32[256,4]{0,1:T(4,128)} %param.15) | copy-start | bytes 12292
  7.2 19.2 %copy-start.5 = (s32[256,3]{0,1:T(4,128)S(1)}, s32[256,3]{0,1:T(4,128)}, u32[]{:S(2)}) copy-start(s32[256,3]{0,1:T(4,128)} %param.14) | copy-start | bytes 9220
  7.2 19.7 %copy-start.7 = (s32[256,3]{0,1:T(4,128)S(1)}, s32[256,3]{0,1:T(4,128)}, u32[]{:S(2)}) copy-start(s32[256,3]{0,1:T(4,128)} %param.13) | copy-start | bytes 9220
  7.2 329.7 %reduce-scatter.2.cloned.1.call-start = ((), (), s32[]{:S(2)}) async-start(), calls=%async_computation.1 | async-start | bytes 1572864 | tf_op jit(solution)/shard_map/reduce_scatter | solution.py:112
  9.8 121.3 %collective-permute-start.5 = (bf16[4,1,8,1024]{3,2,1,0:T(8,128)(2,1)}, bf16[4,1,8,1024]{3,2,1,0:T(8,128)(2,1)}, u32[]{:S(2)}, u32[]{:S(2)}) collective-permute-start(bf16[4,1,8,1024]{3,2,1,0:T(8,128)(2,1)} %get-tuple-element.83), channel_id=1, source_target_pairs={{8,0},{16,8},{24,16},{32,24},{40,32},{48,40},{56,48},{9,1},{17,9},... | collective-permute-start | bytes 196616 | tf_op jit(solution)/shard_map/ppermute | solution.py:17
  11.0 121.3 %collective-permute-start.4 = (bf16[4,1,8,1024]{3,2,1,0:T(8,128)(2,1)}, bf16[4,1,8,1024]{3,2,1,0:T(8,128)(2,1)}, u32[]{:S(2)}, u32[]{:S(2)}) collective-permute-start(bf16[4,1,8,1024]{3,2,1,0:T(8,128)(2,1)} %get-tuple-element.82), channel_id=1, source_target_pairs={{0,8},{8,16},{16,24},{24,32},{32,40},{40,48},{48,56},{1,9},{9,17},... | collective-permute-start | bytes 196616 | tf_op jit(solution)/shard_map/ppermute | solution.py:16
  17.0 139.7 %collective-permute-start.1 = (f32[4,1,8,1024]{3,2,1,0:T(8,128)}, f32[4,1,8,1024]{3,2,1,0:T(8,128)S(1)}, u32[]{:S(2)}, u32[]{:S(2)}) collective-permute-start(f32[4,1,8,1024]{3,2,1,0:T(8,128)} %get-tuple-element.66), channel_id=1, source_target_pairs={{0,8},{8,16},{16,24},{24,32},{32,40},{40,48},{48,56},{1,9},{9,17},... | collective-permute-start | bytes 393224 | tf_op jit(solution)/shard_map/ppermute | solution.py:16
  20.6 139.2 %collective-permute-start = (f32[4,1,8,1024]{3,2,1,0:T(8,128)}, f32[4,1,8,1024]{3,2,1,0:T(8,128)}, u32[]{:S(2)}, u32[]{:S(2)}) collective-permute-start(f32[4,1,8,1024]{3,2,1,0:T(8,128)} %get-tuple-element.67), channel_id=1, source_target_pairs={{8,0},{16,8},{24,16},{32,24},{40,32},{48,40},{56,48},{9,1},{17,9},... | collective-permute-start | bytes 393224 | tf_op jit(solution)/shard_map/ppermute | solution.py:17
  22.6 112.2 %collective-permute-start.17 = (bf16[4,1,8,1024]{3,2,1,0:T(8,128)(2,1)}, bf16[4,1,8,1024]{3,2,1,0:T(8,128)(2,1)}, u32[]{:S(2)}, u32[]{:S(2)}) collective-permute-start(bf16[4,1,8,1024]{3,2,1,0:T(8,128)(2,1)} %get-tuple-element.81), channel_id=1, source_target_pairs={{8,0},{16,8},{24,16},{32,24},{40,32},{48,40},{56,48},{9,1},{17,9},... | collective-permute-start | bytes 196616 | tf_op jit(solution)/shard_map/ppermute | solution.py:17
  131.1 7.8 %collective-permute-start.16 = (bf16[4,1,8,1024]{3,2,1,0:T(8,128)(2,1)}, bf16[4,1,8,1024]{3,2,1,0:T(8,128)(2,1)S(1)}, u32[]{:S(2)}, u32[]{:S(2)}) collective-permute-start(bf16[4,1,8,1024]{3,2,1,0:T(8,128)(2,1)} %get-tuple-element.80), channel_id=1, source_target_pairs={{0,8},{8,16},{16,24},{24,32},{32,40},{40,48},{48,56},{1,9},{9,17},... | collective-permute-start | bytes 196616 | tf_op jit(solution)/shard_map/ppermute | solution.py:16
  132.4 8.9 %collective-permute-start.29 = (bf16[4,1,8,1024]{3,2,1,0:T(8,128)(2,1)}, bf16[4,1,8,1024]{3,2,1,0:T(8,128)(2,1)S(1)}, u32[]{:S(2)}, u32[]{:S(2)}) collective-permute-start(bf16[4,1,8,1024]{3,2,1,0:T(8,128)(2,1)} %get-tuple-element.79), channel_id=1, source_target_pairs={{8,0},{16,8},{24,16},{32,24},{40,32},{48,40},{56,48},{9,1},{17,9},... | collective-permute-start | bytes 196616 | tf_op jit(solution)/shard_map/ppermute | solution.py:17
  134.9 10.5 %collective-permute-start.28 = (bf16[4,1,8,1024]{3,2,1,0:T(8,128)(2,1)}, bf16[4,1,8,1024]{3,2,1,0:T(8,128)(2,1)S(1)}, u32[]{:S(2)}, u32[]{:S(2)}) collective-permute-start(bf16[4,1,8,1024]{3,2,1,0:T(8,128)(2,1)} %get-tuple-element.78), channel_id=1, source_target_pairs={{0,8},{8,16},{16,24},{24,32},{32,40},{40,48},{48,56},{1,9},{9,17},... | collective-permute-start | bytes 196616 | tf_op jit(solution)/shard_map/ppermute | solution.py:16
  138.9 13.2 %collective-permute-start.41 = (bf16[4,1,8,1024]{3,2,1,0:T(8,128)(2,1)}, bf16[4,1,8,1024]{3,2,1,0:T(8,128)(2,1)S(1)}, u32[]{:S(2)}, u32[]{:S(2)}) collective-permute-start(bf16[4,1,8,1024]{3,2,1,0:T(8,128)(2,1)} %get-tuple-element.77), channel_id=1, source_target_pairs={{8,0},{16,8},{24,16},{32,24},{40,32},{48,40},{56,48},{9,1},{17,9},... | collective-permute-start | bytes 196616 | tf_op jit(solution)/shard_map/ppermute | solution.py:17
  141.3 12.7 %collective-permute-start.40 = (bf16[4,1,8,1024]{3,2,1,0:T(8,128)(2,1)}, bf16[4,1,8,1024]{3,2,1,0:T(8,128)(2,1)S(1)}, u32[]{:S(2)}, u32[]{:S(2)}) collective-permute-start(bf16[4,1,8,1024]{3,2,1,0:T(8,128)(2,1)} %get-tuple-element.76), channel_id=1, source_target_pairs={{0,8},{8,16},{16,24},{24,32},{32,40},{40,48},{48,56},{1,9},{9,17},... | collective-permute-start | bytes 196616 | tf_op jit(solution)/shard_map/ppermute | solution.py:16
  145.3 17.6 %collective-permute-start.7 = (bf16[4,10,1,1024]{3,2,1,0:T(2,128)(2,1)S(1)}, bf16[4,10,1,1024]{3,2,1,0:T(2,128)(2,1)S(1)}, u32[]{:S(2)}, u32[]{:S(2)}) collective-permute-start(bf16[4,10,1,1024]{3,2,1,0:T(2,128)(2,1)S(1)} %get-tuple-element.75), channel_id=1, source_target_pairs={{1,0},{2,1},{3,2},{4,3},{5,4},{6,5},{7,6},{9,8},{10,9},{11,10},{12... | collective-permute-start | bytes 245768 | tf_op jit(solution)/shard_map/ppermute | solution.py:17
  152.1 14.5 %collective-permute-start.6 = (bf16[4,10,1,1024]{3,2,1,0:T(2,128)(2,1)S(1)}, bf16[4,10,1,1024]{3,2,1,0:T(2,128)(2,1)S(1)}, u32[]{:S(2)}, u32[]{:S(2)}) collective-permute-start(bf16[4,10,1,1024]{3,2,1,0:T(2,128)(2,1)S(1)} %get-tuple-element.74), channel_id=1, source_target_pairs={{0,1},{1,2},{2,3},{3,4},{4,5},{5,6},{6,7},{8,9},{9,10},{10,11},{11... | collective-permute-start | bytes 245768 | tf_op jit(solution)/shard_map/ppermute | solution.py:16
  154.0 25.6 %collective-permute-start.19 = (bf16[4,10,1,1024]{3,2,1,0:T(2,128)(2,1)S(1)}, bf16[4,10,1,1024]{3,2,1,0:T(2,128)(2,1)S(1)}, u32[]{:S(2)}, u32[]{:S(2)}) collective-permute-start(bf16[4,10,1,1024]{3,2,1,0:T(2,128)(2,1)S(1)} %get-tuple-element.73), channel_id=1, source_target_pairs={{1,0},{2,1},{3,2},{4,3},{5,4},{6,5},{7,6},{9,8},{10,9},{11,10},{12... | collective-permute-start | bytes 245768 | tf_op jit(solution)/shard_map/ppermute | solution.py:17
  156.7 27.2 %collective-permute-start.18 = (bf16[4,10,1,1024]{3,2,1,0:T(2,128)(2,1)S(1)}, bf16[4,10,1,1024]{3,2,1,0:T(2,128)(2,1)S(1)}, u32[]{:S(2)}, u32[]{:S(2)}) collective-permute-start(bf16[4,10,1,1024]{3,2,1,0:T(2,128)(2,1)S(1)} %get-tuple-element.72), channel_id=1, source_target_pairs={{0,1},{1,2},{2,3},{3,4},{4,5},{5,6},{6,7},{8,9},{9,10},{10,11},{11... | collective-permute-start | bytes 245768 | tf_op jit(solution)/shard_map/ppermute | solution.py:16
  159.8 51.7 %collective-permute-start.31 = (bf16[4,10,1,1024]{3,2,1,0:T(2,128)(2,1)S(1)}, bf16[4,10,1,1024]{3,2,1,0:T(2,128)(2,1)S(1)}, u32[]{:S(2)}, u32[]{:S(2)}) collective-permute-start(bf16[4,10,1,1024]{3,2,1,0:T(2,128)(2,1)S(1)} %get-tuple-element.71), channel_id=1, source_target_pairs={{1,0},{2,1},{3,2},{4,3},{5,4},{6,5},{7,6},{9,8},{10,9},{11,10},{12... | collective-permute-start | bytes 245768 | tf_op jit(solution)/shard_map/ppermute | solution.py:17
  163.0 8.6 %collective-permute-start.3 = (f32[4,10,1,1024]{3,2,1,0:T(1,128)S(1)}, f32[4,10,1,1024]{3,2,1,0:T(1,128)S(1)}, u32[]{:S(2)}, u32[]{:S(2)}) collective-permute-start(f32[4,10,1,1024]{3,2,1,0:T(1,128)S(1)} %get-tuple-element.47), channel_id=1, source_target_pairs={{0,1},{1,2},{2,3},{3,4},{4,5},{5,6},{6,7},{8,9},{9,10},{10,11},{11... | collective-permute-start | bytes 491528 | tf_op jit(solution)/shard_map/ppermute | solution.py:16
  166.6 8.7 %collective-permute-start.2 = (f32[4,10,1,1024]{3,2,1,0:T(1,128)S(1)}, f32[4,10,1,1024]{3,2,1,0:T(1,128)S(1)}, u32[]{:S(2)}, u32[]{:S(2)}) collective-permute-start(f32[4,10,1,1024]{3,2,1,0:T(1,128)S(1)} %get-tuple-element.46), channel_id=1, source_target_pairs={{1,0},{2,1},{3,2},{4,3},{5,4},{6,5},{7,6},{9,8},{10,9},{11,10},{12... | collective-permute-start | bytes 491528 | tf_op jit(solution)/shard_map/ppermute | solution.py:17
  171.5 7.7 %copy-start.1 = (f32[8,8,1024]{2,1,0:T(8,128)S(1)}, f32[8,8,1024]{2,1,0:T(8,128)}, u32[]{:S(2)}) copy-start(f32[8,8,1024]{2,1,0:T(8,128)} %param.8) | copy-start | bytes 786436
  171.5 7.7 %copy-start.4 = (f32[8,8,1024]{2,1,0:T(8,128)S(1)}, f32[8,8,1024]{2,1,0:T(8,128)}, u32[]{:S(2)}) copy-start(f32[8,8,1024]{2,1,0:T(8,128)} %reshape.127) | copy-start | bytes 786436
  171.6 41.9 %collective-permute-start.30 = (bf16[4,10,1,1024]{3,2,1,0:T(2,128)(2,1)S(1)}, bf16[4,10,1,1024]{3,2,1,0:T(2,128)(2,1)S(1)}, u32[]{:S(2)}, u32[]{:S(2)}) collective-permute-start(bf16[4,10,1,1024]{3,2,1,0:T(2,128)(2,1)S(1)} %get-tuple-element.70), channel_id=1, source_target_pairs={{0,1},{1,2},{2,3},{3,4},{4,5},{5,6},{6,7},{8,9},{9,10},{10,11},{11... | collective-permute-start | bytes 245768 | tf_op jit(solution)/shard_map/ppermute | solution.py:16
  175.4 57.7 %collective-permute-start.43 = (bf16[4,10,1,1024]{3,2,1,0:T(2,128)(2,1)S(1)}, bf16[4,10,1,1024]{3,2,1,0:T(2,128)(2,1)S(1)}, u32[]{:S(2)}, u32[]{:S(2)}) collective-permute-start(bf16[4,10,1,1024]{3,2,1,0:T(2,128)(2,1)S(1)} %get-tuple-element.69), channel_id=1, source_target_pairs={{1,0},{2,1},{3,2},{4,3},{5,4},{6,5},{7,6},{9,8},{10,9},{11,10},{12... | collective-permute-start | bytes 245768 | tf_op jit(solution)/shard_map/ppermute | solution.py:17
  179.6 7.1 %collective-permute-start.9 = (f32[1,8,1024]{2,1,0:T(8,128)S(1)}, f32[1,8,1024]{2,1,0:T(8,128)S(1)}, u32[]{:S(2)}, u32[]{:S(2)}) collective-permute-start(f32[1,8,1024]{2,1,0:T(8,128)S(1)} %get-tuple-element.110), channel_id=1, source_target_pairs={{0,8},{8,16},{16,24},{24,32},{32,40},{40,48},{48,56},{1,9},{9,17},... | collective-permute-start | bytes 98312 | tf_op jit(solution)/shard_map/ppermute | solution.py:16
  183.9 4.7 %collective-permute-start.8 = (f32[1,8,1024]{2,1,0:T(8,128)S(1)}, f32[1,8,1024]{2,1,0:T(8,128)S(1)}, u32[]{:S(2)}, u32[]{:S(2)}) collective-permute-start(f32[1,8,1024]{2,1,0:T(8,128)S(1)} %get-tuple-element.111), channel_id=1, source_target_pairs={{8,0},{16,8},{24,16},{32,24},{40,32},{48,40},{56,48},{9,1},{17,9},... | collective-permute-start | bytes 98312 | tf_op jit(solution)/shard_map/ppermute | solution.py:17
  188.6 7.6 %collective-permute-start.11 = (f32[10,1,1024]{2,1,0:T(1,128)S(1)}, f32[10,1,1024]{2,1,0:T(1,128)S(1)}, u32[]{:S(2)}, u32[]{:S(2)}) collective-permute-start(f32[10,1,1024]{2,1,0:T(1,128)S(1)} %get-tuple-element.99), channel_id=1, source_target_pairs={{0,1},{1,2},{2,3},{3,4},{4,5},{5,6},{6,7},{8,9},{9,10},{10,11},{11... | collective-permute-start | bytes 122888 | tf_op jit(solution)/shard_map/ppermute | solution.py:16
  193.7 5.3 %collective-permute-start.10 = (f32[10,1,1024]{2,1,0:T(1,128)S(1)}, f32[10,1,1024]{2,1,0:T(1,128)S(1)}, u32[]{:S(2)}, u32[]{:S(2)}) collective-permute-start(f32[10,1,1024]{2,1,0:T(1,128)S(1)} %get-tuple-element.98), channel_id=1, source_target_pairs={{1,0},{2,1},{3,2},{4,3},{5,4},{6,5},{7,6},{9,8},{10,9},{11,10},{12... | collective-permute-start | bytes 122888 | tf_op jit(solution)/shard_map/ppermute | solution.py:17
  199.7 4.5 %collective-permute-start.13 = (f32[4,1,8,1024]{3,2,1,0:T(8,128)S(1)}, f32[4,1,8,1024]{3,2,1,0:T(8,128)S(1)}, u32[]{:S(2)}, u32[]{:S(2)}) collective-permute-start(f32[4,1,8,1024]{3,2,1,0:T(8,128)S(1)} %get-tuple-element.61), channel_id=1, source_target_pairs={{0,8},{8,16},{16,24},{24,32},{32,40},{40,48},{48,56},{1,9},{9,17},... | collective-permute-start | bytes 393224 | tf_op jit(solution)/shard_map/ppermute | solution.py:16
  202.3 5.8 %collective-permute-start.12 = (f32[4,1,8,1024]{3,2,1,0:T(8,128)S(1)}, f32[4,1,8,1024]{3,2,1,0:T(8,128)S(1)}, u32[]{:S(2)}, u32[]{:S(2)}) collective-permute-start(f32[4,1,8,1024]{3,2,1,0:T(8,128)S(1)} %get-tuple-element.62), channel_id=1, source_target_pairs={{8,0},{16,8},{24,16},{32,24},{40,32},{48,40},{56,48},{9,1},{17,9},... | collective-permute-start | bytes 393224 | tf_op jit(solution)/shard_map/ppermute | solution.py:17
  204.2 28.8 %collective-permute-start.42 = (bf16[4,10,1,1024]{3,2,1,0:T(2,128)(2,1)S(1)}, bf16[4,10,1,1024]{3,2,1,0:T(2,128)(2,1)S(1)}, u32[]{:S(2)}, u32[]{:S(2)}) collective-permute-start(bf16[4,10,1,1024]{3,2,1,0:T(2,128)(2,1)S(1)} %get-tuple-element.68), channel_id=1, source_target_pairs={{0,1},{1,2},{2,3},{3,4},{4,5},{5,6},{6,7},{8,9},{9,10},{10,11},{11... | collective-permute-start | bytes 245768 | tf_op jit(solution)/shard_map/ppermute | solution.py:16
  208.3 5.9 %collective-permute-start.15 = (f32[4,10,1,1024]{3,2,1,0:T(1,128)S(1)}, f32[4,10,1,1024]{3,2,1,0:T(1,128)S(1)}, u32[]{:S(2)}, u32[]{:S(2)}) collective-permute-start(f32[4,10,1,1024]{3,2,1,0:T(1,128)S(1)} %get-tuple-element.43), channel_id=1, source_target_pairs={{0,1},{1,2},{2,3},{3,4},{4,5},{5,6},{6,7},{8,9},{9,10},{10,11},{11... | collective-permute-start | bytes 491528 | tf_op jit(solution)/shard_map/ppermute | solution.py:16
  211.6 6.6 %collective-permute-start.14 = (f32[4,10,1,1024]{3,2,1,0:T(1,128)S(1)}, f32[4,10,1,1024]{3,2,1,0:T(1,128)S(1)}, u32[]{:S(2)}, u32[]{:S(2)}) collective-permute-start(f32[4,10,1,1024]{3,2,1,0:T(1,128)S(1)} %get-tuple-element.42), channel_id=1, source_target_pairs={{1,0},{2,1},{3,2},{4,3},{5,4},{6,5},{7,6},{9,8},{10,9},{11,10},{12... | collective-permute-start | bytes 491528 | tf_op jit(solution)/shard_map/ppermute | solution.py:17
  214.2 5.1 %copy-start.3 = (f32[8,8,1024]{2,1,0:T(8,128)S(1)}, f32[8,8,1024]{2,1,0:T(8,128)}, u32[]{:S(2)}) copy-start(f32[8,8,1024]{2,1,0:T(8,128)} %reshape.128) | copy-start | bytes 786436
  219.6 5.5 %collective-permute-start.21 = (f32[1,8,1024]{2,1,0:T(8,128)S(1)}, f32[1,8,1024]{2,1,0:T(8,128)S(1)}, u32[]{:S(2)}, u32[]{:S(2)}) collective-permute-start(f32[1,8,1024]{2,1,0:T(8,128)S(1)} %get-tuple-element.107), channel_id=1, source_target_pairs={{0,8},{8,16},{16,24},{24,32},{32,40},{40,48},{48,56},{1,9},{9,17},... | collective-permute-start | bytes 98312 | tf_op jit(solution)/shard_map/ppermute | solution.py:16
  223.2 4.7 %collective-permute-start.20 = (f32[1,8,1024]{2,1,0:T(8,128)S(1)}, f32[1,8,1024]{2,1,0:T(8,128)S(1)}, u32[]{:S(2)}, u32[]{:S(2)}) collective-permute-start(f32[1,8,1024]{2,1,0:T(8,128)S(1)} %get-tuple-element.108), channel_id=1, source_target_pairs={{8,0},{16,8},{24,16},{32,24},{40,32},{48,40},{56,48},{9,1},{17,9},... | collective-permute-start | bytes 98312 | tf_op jit(solution)/shard_map/ppermute | solution.py:17
  228.0 5.8 %collective-permute-start.23 = (f32[10,1,1024]{2,1,0:T(1,128)S(1)}, f32[10,1,1024]{2,1,0:T(1,128)S(1)}, u32[]{:S(2)}, u32[]{:S(2)}) collective-permute-start(f32[10,1,1024]{2,1,0:T(1,128)S(1)} %get-tuple-element.95), channel_id=1, source_target_pairs={{0,1},{1,2},{2,3},{3,4},{4,5},{5,6},{6,7},{8,9},{9,10},{10,11},{11... | collective-permute-start | bytes 122888 | tf_op jit(solution)/shard_map/ppermute | solution.py:16
  231.1 5.3 %collective-permute-start.22 = (f32[10,1,1024]{2,1,0:T(1,128)S(1)}, f32[10,1,1024]{2,1,0:T(1,128)S(1)}, u32[]{:S(2)}, u32[]{:S(2)}) collective-permute-start(f32[10,1,1024]{2,1,0:T(1,128)S(1)} %get-tuple-element.94), channel_id=1, source_target_pairs={{1,0},{2,1},{3,2},{4,3},{5,4},{6,5},{7,6},{9,8},{10,9},{11,10},{12... | collective-permute-start | bytes 122888 | tf_op jit(solution)/shard_map/ppermute | solution.py:17
  237.2 6.2 %collective-permute-start.25 = (f32[4,1,8,1024]{3,2,1,0:T(8,128)S(1)}, f32[4,1,8,1024]{3,2,1,0:T(8,128)S(1)}, u32[]{:S(2)}, u32[]{:S(2)}) collective-permute-start(f32[4,1,8,1024]{3,2,1,0:T(8,128)S(1)} %get-tuple-element.56), channel_id=1, source_target_pairs={{0,8},{8,16},{16,24},{24,32},{32,40},{40,48},{48,56},{1,9},{9,17},... | collective-permute-start | bytes 393224 | tf_op jit(solution)/shard_map/ppermute | solution.py:16
  241.5 6.2 %collective-permute-start.24 = (f32[4,1,8,1024]{3,2,1,0:T(8,128)S(1)}, f32[4,1,8,1024]{3,2,1,0:T(8,128)S(1)}, u32[]{:S(2)}, u32[]{:S(2)}) collective-permute-start(f32[4,1,8,1024]{3,2,1,0:T(8,128)S(1)} %get-tuple-element.57), channel_id=1, source_target_pairs={{8,0},{16,8},{24,16},{32,24},{40,32},{48,40},{56,48},{9,1},{17,9},... | collective-permute-start | bytes 393224 | tf_op jit(solution)/shard_map/ppermute | solution.py:17
  247.9 6.4 %collective-permute-start.27 = (f32[4,10,1,1024]{3,2,1,0:T(1,128)S(1)}, f32[4,10,1,1024]{3,2,1,0:T(1,128)S(1)}, u32[]{:S(2)}, u32[]{:S(2)}) collective-permute-start(f32[4,10,1,1024]{3,2,1,0:T(1,128)S(1)} %get-tuple-element.39), channel_id=1, source_target_pairs={{0,1},{1,2},{2,3},{3,4},{4,5},{5,6},{6,7},{8,9},{9,10},{10,11},{11... | collective-permute-start | bytes 491528 | tf_op jit(solution)/shard_map/ppermute | solution.py:16
  251.0 6.6 %collective-permute-start.26 = (f32[4,10,1,1024]{3,2,1,0:T(1,128)S(1)}, f32[4,10,1,1024]{3,2,1,0:T(1,128)S(1)}, u32[]{:S(2)}, u32[]{:S(2)}) collective-permute-start(f32[4,10,1,1024]{3,2,1,0:T(1,128)S(1)} %get-tuple-element.38), channel_id=1, source_target_pairs={{1,0},{2,1},{3,2},{4,3},{5,4},{6,5},{7,6},{9,8},{10,9},{11,10},{12... | collective-permute-start | bytes 491528 | tf_op jit(solution)/shard_map/ppermute | solution.py:17
  254.3 4.4 %copy-start.2 = (f32[8,8,1024]{2,1,0:T(8,128)S(1)}, f32[8,8,1024]{2,1,0:T(8,128)}, u32[]{:S(2)}) copy-start(f32[8,8,1024]{2,1,0:T(8,128)} %reshape.129) | copy-start | bytes 786436
  259.1 5.5 %collective-permute-start.33 = (f32[1,8,1024]{2,1,0:T(8,128)S(1)}, f32[1,8,1024]{2,1,0:T(8,128)S(1)}, u32[]{:S(2)}, u32[]{:S(2)}) collective-permute-start(f32[1,8,1024]{2,1,0:T(8,128)S(1)} %get-tuple-element.104), channel_id=1, source_target_pairs={{0,8},{8,16},{16,24},{24,32},{32,40},{40,48},{48,56},{1,9},{9,17},... | collective-permute-start | bytes 98312 | tf_op jit(solution)/shard_map/ppermute | solution.py:16
  263.0 4.7 %collective-permute-start.32 = (f32[1,8,1024]{2,1,0:T(8,128)S(1)}, f32[1,8,1024]{2,1,0:T(8,128)S(1)}, u32[]{:S(2)}, u32[]{:S(2)}) collective-permute-start(f32[1,8,1024]{2,1,0:T(8,128)S(1)} %get-tuple-element.105), channel_id=1, source_target_pairs={{8,0},{16,8},{24,16},{32,24},{40,32},{48,40},{56,48},{9,1},{17,9},... | collective-permute-start | bytes 98312 | tf_op jit(solution)/shard_map/ppermute | solution.py:17
  267.7 5.3 %collective-permute-start.35 = (f32[10,1,1024]{2,1,0:T(1,128)S(1)}, f32[10,1,1024]{2,1,0:T(1,128)S(1)}, u32[]{:S(2)}, u32[]{:S(2)}) collective-permute-start(f32[10,1,1024]{2,1,0:T(1,128)S(1)} %get-tuple-element.91), channel_id=1, source_target_pairs={{0,1},{1,2},{2,3},{3,4},{4,5},{5,6},{6,7},{8,9},{9,10},{10,11},{11... | collective-permute-start | bytes 122888 | tf_op jit(solution)/shard_map/ppermute | solution.py:16
  270.9 5.3 %collective-permute-start.34 = (f32[10,1,1024]{2,1,0:T(1,128)S(1)}, f32[10,1,1024]{2,1,0:T(1,128)S(1)}, u32[]{:S(2)}, u32[]{:S(2)}) collective-permute-start(f32[10,1,1024]{2,1,0:T(1,128)S(1)} %get-tuple-element.90), channel_id=1, source_target_pairs={{1,0},{2,1},{3,2},{4,3},{5,4},{6,5},{7,6},{9,8},{10,9},{11,10},{12... | collective-permute-start | bytes 122888 | tf_op jit(solution)/shard_map/ppermute | solution.py:17
  276.9 5.4 %collective-permute-start.37 = (f32[4,1,8,1024]{3,2,1,0:T(8,128)S(1)}, f32[4,1,8,1024]{3,2,1,0:T(8,128)S(1)}, u32[]{:S(2)}, u32[]{:S(2)}) collective-permute-start(f32[4,1,8,1024]{3,2,1,0:T(8,128)S(1)} %get-tuple-element.51), channel_id=1, source_target_pairs={{0,8},{8,16},{16,24},{24,32},{32,40},{40,48},{48,56},{1,9},{9,17},... | collective-permute-start | bytes 393224 | tf_op jit(solution)/shard_map/ppermute | solution.py:16
  280.4 5.7 %collective-permute-start.36 = (f32[4,1,8,1024]{3,2,1,0:T(8,128)S(1)}, f32[4,1,8,1024]{3,2,1,0:T(8,128)S(1)}, u32[]{:S(2)}, u32[]{:S(2)}) collective-permute-start(f32[4,1,8,1024]{3,2,1,0:T(8,128)S(1)} %get-tuple-element.52), channel_id=1, source_target_pairs={{8,0},{16,8},{24,16},{32,24},{40,32},{48,40},{56,48},{9,1},{17,9},... | collective-permute-start | bytes 393224 | tf_op jit(solution)/shard_map/ppermute | solution.py:17
  286.3 5.9 %collective-permute-start.39 = (f32[4,10,1,1024]{3,2,1,0:T(1,128)S(1)}, f32[4,10,1,1024]{3,2,1,0:T(1,128)S(1)}, u32[]{:S(2)}, u32[]{:S(2)}) collective-permute-start(f32[4,10,1,1024]{3,2,1,0:T(1,128)S(1)} %get-tuple-element.35), channel_id=1, source_target_pairs={{0,1},{1,2},{2,3},{3,4},{4,5},{5,6},{6,7},{8,9},{9,10},{10,11},{11... | collective-permute-start | bytes 491528 | tf_op jit(solution)/shard_map/ppermute | solution.py:16
  290.0 6.6 %collective-permute-start.38 = (f32[4,10,1,1024]{3,2,1,0:T(1,128)S(1)}, f32[4,10,1,1024]{3,2,1,0:T(1,128)S(1)}, u32[]{:S(2)}, u32[]{:S(2)}) collective-permute-start(f32[4,10,1,1024]{3,2,1,0:T(1,128)S(1)} %get-tuple-element.34), channel_id=1, source_target_pairs={{1,0},{2,1},{3,2},{4,3},{5,4},{6,5},{7,6},{9,8},{10,9},{11,10},{12... | collective-permute-start | bytes 491528 | tf_op jit(solution)/shard_map/ppermute | solution.py:17
  298.1 4.5 %collective-permute-start.45 = (f32[1,8,1024]{2,1,0:T(8,128)S(1)}, f32[1,8,1024]{2,1,0:T(8,128)S(1)}, u32[]{:S(2)}, u32[]{:S(2)}) collective-permute-start(f32[1,8,1024]{2,1,0:T(8,128)S(1)} %get-tuple-element.101), channel_id=1, source_target_pairs={{0,8},{8,16},{16,24},{24,32},{32,40},{40,48},{48,56},{1,9},{9,17},... | collective-permute-start | bytes 98312 | tf_op jit(solution)/shard_map/ppermute | solution.py:16
  300.9 4.7 %collective-permute-start.44 = (f32[1,8,1024]{2,1,0:T(8,128)S(1)}, f32[1,8,1024]{2,1,0:T(8,128)S(1)}, u32[]{:S(2)}, u32[]{:S(2)}) collective-permute-start(f32[1,8,1024]{2,1,0:T(8,128)S(1)} %get-tuple-element.102), channel_id=1, source_target_pairs={{8,0},{16,8},{24,16},{32,24},{40,32},{48,40},{56,48},{9,1},{17,9},... | collective-permute-start | bytes 98312 | tf_op jit(solution)/shard_map/ppermute | solution.py:17
  305.7 5.3 %collective-permute-start.47 = (f32[10,1,1024]{2,1,0:T(1,128)S(1)}, f32[10,1,1024]{2,1,0:T(1,128)S(1)}, u32[]{:S(2)}, u32[]{:S(2)}) collective-permute-start(f32[10,1,1024]{2,1,0:T(1,128)S(1)} %get-tuple-element.87), channel_id=1, source_target_pairs={{0,1},{1,2},{2,3},{3,4},{4,5},{5,6},{6,7},{8,9},{9,10},{10,11},{11... | collective-permute-start | bytes 122888 | tf_op jit(solution)/shard_map/ppermute | solution.py:16
  308.8 5.3 %collective-permute-start.46 = (f32[10,1,1024]{2,1,0:T(1,128)S(1)}, f32[10,1,1024]{2,1,0:T(1,128)S(1)}, u32[]{:S(2)}, u32[]{:S(2)}) collective-permute-start(f32[10,1,1024]{2,1,0:T(1,128)S(1)} %get-tuple-element.86), channel_id=1, source_target_pairs={{1,0},{2,1},{3,2},{4,3},{5,4},{6,5},{7,6},{9,8},{10,9},{11,10},{12... | collective-permute-start | bytes 122888 | tf_op jit(solution)/shard_map/ppermute | solution.py:17
Sparse Core Ops, SparseCore 0:
  317.0 19.8 reduce-scatter.1
